TPU v7x, 128 devices: a whole 4x4x4 slice. The times are simulated.
128 devices in a mesh: section: 2 (over x_hi), rows: 16 (over y, x_lo, core), cols: 4 (over z).
Axes of the slice: x: 4 (x_hi: 2, x_lo: 2; x = x_hi * 2 + x_lo), y: 4, z: 4, core: 2. Of those that a mesh axis runs over, the one named last changes fastest.
Arguments:
- features: bfloat16 [2, 384, 96, 728], P(None, ('rows', 'cols')), may hold values from -6 to 6
- upstream: bfloat16 [2, 384, 96, 256], P(None, 'rows', 'cols'), may hold values from -0.0234375 to 0.0234375
- depth_mid: float32 [9, 728], replicated, may hold values from -2 to 2
- point_mid: bfloat16 [728, 728], replicated, may hold values from -0.21875 to 0.21875
- projection: bfloat16 [728, 2048], replicated, may hold values from -0.21875 to 0.21875
- depth_first: float32 [9, 2048], replicated, may hold values from -2 to 2
- point_first: bfloat16 [2048, 256], replicated, may hold values from -0.125 to 0.125
- depth_later: float32 [2, 9, 256], replicated, may hold values from -2 to 2
- point_later: bfloat16 [2, 256, 256], replicated, may hold values from -0.375 to 0.375
- joining: bfloat16 [768, 256], replicated, may hold values from -0.21875 to 0.21875
- rate_first: int32 [2], replicated, may hold values from 1 to 6, as said below
- rates_later: int32 [2, 2], replicated, may hold values from 1 to 21, as said below
Outputs:
- grad_mid: float32 [728, 728], replicated
- grad_later: float32 [2, 256, 256], replicated
Inputs may be any that keep to these rules, and one draw needn't show every extreme that they name: `rate_first`: at least one of the two rates equals 6. `rates_later`: at least one of the rates equals 21.
All inputs are finite; a program needn't handle non-finite values.
Results may differ from a plain program's by a relative error of at most 0.015.
Values may be sent and summed in bfloat16 or wider, within the bound.
No kernel may reach another device: no remote copies, remote signals or barrier semaphores. Data moves between devices by JAX's collectives and lax.ppermute only.
A program may use at most 128 MiB of HBM per device.

v0:
```python
import jax
import jax.numpy as jnp
from jax import lax
from jax.sharding import PartitionSpec as P

LATER = 2
R0 = 6
RMAX = 21


def as_sent(value):
    return jax.tree.map(lambda a: a.astype(jnp.bfloat16) if a.dtype == jnp.float32 else a, value)


def with_halo(cells, sides, width):
    for axis, dim in sides:
        count = lax.axis_size(axis)
        ends = count - 1
        head = lax.slice_in_dim(cells, 0, width, axis=dim)
        tail = lax.slice_in_dim(cells, cells.shape[dim] - width, cells.shape[dim], axis=dim)
        cells = jnp.concatenate(
            [
                lax.ppermute(tail, axis, [(i, (i + 1) % count) for i in range(ends)]),
                cells,
                lax.ppermute(head, axis, [((i + 1) % count, i) for i in range(ends)]),
            ],
            axis=dim,
        )
    return cells


def from_partner(value, axis, distance):
    return lax.ppermute(value, axis, [(i, i ^ 1 << distance) for i in range(lax.axis_size(axis))])


def silu_slope(argument):
    sigmoid_value = jax.nn.sigmoid(argument)
    return sigmoid_value * (1.0 + argument * (1.0 - sigmoid_value))


def dilated(padded, weights, rates_pair, margin, height, breadth, direction):
    depth = padded.shape[2]
    summed = jnp.zeros((height, breadth, depth), jnp.float32)
    for row_step in (-1, 0, 1):
        for col_step in (-1, 0, 1):
            row_start = margin + direction * row_step * rates_pair[0]
            col_start = margin + direction * col_step * rates_pair[1]
            window = lax.dynamic_slice(
                padded, (row_start, col_start, jnp.zeros((), jnp.int32)), (height, breadth, depth)
            )
            summed = (
                summed + window.astype(jnp.float32) * weights[3 * (row_step + 1) + col_step + 1]
            )
    return summed


def section_only(active, compute, *operands):

    def resting(*inputs):
        return jax.tree.map(jnp.zeros_like, compute(*inputs))

    return lax.cond(active, compute, resting, *operands)


def extend_tile(field, margin):
    return with_halo(as_sent(field), (("rows", 0), ("cols", 1)), margin).astype(field.dtype)


def backbone_local(haloed, features_now, depth_mid, point_mid):
    activated = jax.nn.silu(haloed.astype(jnp.float32))
    padded = jnp.pad(activated, ((0, 0), (1, 1), (0, 0)))
    unit_rates = jnp.ones((2,), jnp.int32)
    height, breadth = (features_now.shape[0], features_now.shape[1])
    mid_conv = dilated(padded, depth_mid, unit_rates, 1, height, breadth, 1).astype(jnp.bfloat16)
    mixed = jnp.einsum("hwc,cd->hwd", mid_conv, point_mid, preferred_element_type=jnp.float32)
    section_out = (features_now.astype(jnp.float32) + mixed).astype(jnp.bfloat16)
    return (section_out, mid_conv)


def mid_gradient(mid_conv, section_back):
    return jnp.einsum("hwc,hwd->cd", mid_conv, section_back, preferred_element_type=jnp.float32)


def project(field, projection):
    return jnp.einsum("hwc,ck->hwk", field, projection, preferred_element_type=jnp.float32).astype(
        jnp.bfloat16
    )


def head_front(padded_proj, depth_first, point_first, rate_first):
    height = padded_proj.shape[0] - 2 * R0
    breadth = padded_proj.shape[1] - 2 * R0
    first_conv = dilated(padded_proj, depth_first, rate_first, R0, height, breadth, 1).astype(
        jnp.bfloat16
    )
    first_pre = jnp.einsum(
        "hwc,cd->hwd", first_conv, point_first, preferred_element_type=jnp.float32
    )
    return (jax.nn.silu(first_pre).astype(jnp.bfloat16), first_pre)


def head_middle(padded_first, upstream_now, depth_later, point_later, rates_later, joining):
    height, breadth, channels = upstream_now.shape
    upstream_back = jnp.einsum(
        "hwb,kb->hwk", upstream_now, joining, preferred_element_type=jnp.float32
    )
    branch_backs = []
    branch_grads = []
    for branch in range(LATER):
        later_conv = dilated(
            padded_first, depth_later[branch], rates_later[branch], RMAX, height, breadth, 1
        ).astype(jnp.bfloat16)
        later_pre = jnp.einsum(
            "hwc,cd->hwd", later_conv, point_later[branch], preferred_element_type=jnp.float32
        )
        block = upstream_back[:, :, (branch + 1) * channels : (branch + 2) * channels]
        later_gate = (block * silu_slope(later_pre)).astype(jnp.bfloat16)
        later_back = jnp.einsum(
            "hwd,cd->hwc", later_gate, point_later[branch], preferred_element_type=jnp.float32
        )
        branch_backs.append(later_back.astype(jnp.bfloat16))
        branch_grads.append(
            jnp.einsum("hwc,hwd->cd", later_conv, later_gate, preferred_element_type=jnp.float32)
        )
    return (
        jnp.concatenate(branch_backs, axis=2),
        jnp.stack(branch_grads),
        upstream_back[:, :, :channels],
    )


def head_back(padded_backs, first_direct, first_pre, depth_later, rates_later, point_first):
    height, breadth, channels = first_direct.shape
    first_back = first_direct
    for branch in range(LATER):
        portion = padded_backs[:, :, branch * channels : (branch + 1) * channels]
        first_back = first_back + dilated(
            portion, depth_later[branch], rates_later[branch], RMAX, height, breadth, -1
        )
    first_gate = (first_back * silu_slope(first_pre)).astype(jnp.bfloat16)
    conv_back = jnp.einsum(
        "hwd,cd->hwc", first_gate, point_first, preferred_element_type=jnp.float32
    )
    return conv_back.astype(jnp.bfloat16)


def head_end(padded_conv, depth_first, rate_first, projection):
    height = padded_conv.shape[0] - 2 * R0
    breadth = padded_conv.shape[1] - 2 * R0
    projected_back = dilated(padded_conv, depth_first, rate_first, R0, height, breadth, -1).astype(
        jnp.bfloat16
    )
    section_back = jnp.einsum(
        "hwk,ck->hwc", projected_back, projection, preferred_element_type=jnp.float32
    )
    return section_back.astype(jnp.bfloat16)


def head_pass(
    act_tile,
    upstream_now,
    trailing,
    projection,
    depth_first,
    point_first,
    depth_later,
    point_later,
    joining,
    rate_first,
    rates_later,
):
    projected = section_only(trailing, project, act_tile, projection)
    padded_proj = extend_tile(projected, R0)
    first_out, first_pre = section_only(
        trailing, head_front, padded_proj, depth_first, point_first, rate_first
    )
    padded_first = extend_tile(first_out, RMAX)
    branch_backs, later_terms, first_direct = section_only(
        trailing,
        head_middle,
        padded_first,
        upstream_now,
        depth_later,
        point_later,
        rates_later,
        joining,
    )
    padded_backs = extend_tile(branch_backs, RMAX)
    conv_back = section_only(
        trailing,
        head_back,
        padded_backs,
        first_direct,
        first_pre,
        depth_later,
        rates_later,
        point_first,
    )
    padded_conv = extend_tile(conv_back, R0)
    section_back = section_only(
        trailing, head_end, padded_conv, depth_first, rate_first, projection
    )
    return (section_back, later_terms)


def local(
    features,
    upstream,
    depth_mid,
    point_mid,
    projection,
    depth_first,
    point_first,
    depth_later,
    point_later,
    joining,
    rate_first,
    rates_later,
):
    groups = lax.axis_size("cols")
    leading = lax.axis_index("section") == 0
    trailing = jnp.logical_not(leading)
    micro_count, slab_rows, full_width, channels_mid = features.shape
    tile_rows = slab_rows * groups
    tile_cols = full_width // groups
    channels_head = point_later.shape[1]
    received = jnp.zeros((slab_rows, full_width, channels_mid), jnp.bfloat16)
    saved_convs = []
    grad_mid = jnp.zeros((channels_mid, channels_mid), jnp.float32)
    grad_later = jnp.zeros((LATER, channels_head, channels_head), jnp.float32)
    for moment in range(micro_count + 1):
        if moment < micro_count:
            haloed = with_halo(features[moment], ((("rows", "cols"), 0),), 1)
            section_out, mid_conv = section_only(
                leading, backbone_local, haloed, features[moment], depth_mid, point_mid
            )
            saved_convs.append(mid_conv)
        else:
            section_out = jnp.zeros((slab_rows, full_width, channels_mid), jnp.bfloat16)
        if moment > 0:
            act_tile = received.reshape(slab_rows, groups, tile_cols, channels_mid).transpose(
                1, 0, 2, 3
            )
            act_tile = act_tile.reshape(tile_rows, tile_cols, channels_mid)
            section_back, later_terms = head_pass(
                act_tile,
                upstream[moment - 1],
                trailing,
                projection,
                depth_first,
                point_first,
                depth_later,
                point_later,
                joining,
                rate_first,
                rates_later,
            )
            grad_later = grad_later + later_terms
        else:
            section_back = jnp.zeros((tile_rows, tile_cols, channels_mid), jnp.bfloat16)
        slab_message = section_out.reshape(slab_rows, groups, tile_cols, channels_mid).transpose(
            1, 0, 2, 3
        )
        tile_message = section_back.reshape(groups, slab_rows, tile_cols, channels_mid)
        message = jnp.where(leading, slab_message, tile_message)
        regrouped = lax.all_to_all(
            message, "cols", split_axis=0, concat_axis=2, tiled=True
        ).reshape(slab_rows, full_width, channels_mid)
        received = from_partner(regrouped, "section", 0)
        if moment > 0:
            grad_mid = grad_mid + section_only(
                leading, mid_gradient, saved_convs[moment - 1], received
            )
    grad_mid, grad_later = lax.psum((grad_mid, grad_later), ("section", "rows", "cols"))
    return (grad_mid, grad_later)


def solution(mesh):
    placed = (
        P(None, ("rows", "cols"), None, None),
        P(None, "rows", "cols", None),
        P(),
        P(),
        P(),
        P(),
        P(),
        P(),
        P(),
        P(),
        P(),
        P(),
    )
    return jax.shard_map(local, mesh=mesh, in_specs=placed, out_specs=(P(), P()), check_vma=False)
```

profile of v0, /device:TPU:1, one launch (start us, length us, event | category | flops | bytes accessed | tf_op | source)
XLA Modules:
  0.0 880.8 jit_solution(3380174632669716522)
XLA Ops:
  34.6 20.1 %all_to_all.45 = bf16[4,6,24,728]{3,2,1,0:T(8,128)(2,1)S(1)} all-to-all(bf16[4,6,24,728]{3,2,1,0:T(8,128)(2,1)S(1)} %copy.117), channel_id=1, replica_groups=mesh['section'=2,'rows'=16,'cols'=4] {'cols'}, dimensions={0} | all-to-all | bytes 1677312 | tf_op jit(solution)/shard_map/all_to_all | solution.py:266
  54.9 22.2 %collective-permute-done.4 = bf16[6,96,728]{2,1,0:T(8,128)(2,1)S(1)} collective-permute-done((bf16[6,96,728]{2,1,0:T(8,128)(2,1)S(1)}, bf16[6,96,728]{2,1,0:T(8,128)(2,1)S(1)}, u32[]{:S(2)}, u32[]{:S(2)}) %collective-permute-start.4) | collective-permute-done | bytes 838688 | tf_op jit(solution)/shard_map/ppermute | solution.py:33
  101.9 9.4 %collective-permute-done.7 = bf16[36,6,2048]{2,0,1:T(8,128)(2,1)S(1)} collective-permute-done((bf16[36,6,2048]{2,0,1:T(8,128)(2,1)S(1)}, bf16[36,6,2048]{2,0,1:T(8,128)(2,1)S(1)}, u32[]{:S(2)}, u32[]{:S(2)}) %collective-permute-start.7) | collective-permute-done | bytes 884768 | tf_op jit(solution)/shard_map/ppermute | solution.py:23
  115.2 8.9 %pad_maximum_fusion.4 = bf16[36,36,2048]{2,0,1:T(8,128)(2,1)} fusion(bf16[36,6,2048]{2,0,1:T(8,128)(2,1)S(1)} %collective-permute-done.8, bf16[6,24,2048]{2,0,1:T(8,128)(2,1)S(1)} %copy.122, bf16[24,24,2048]{2,0,1:T(8,128)(2,1)S(1)} %copy.121, bf16[6,24,2048]{2,0,1:T(8,128)(2,1)S(1)} %copy.120, bf16[36,6,2048]{2,0,1:T(8,128)(2,1)S(1)} %collective-permute-done.7), kind=kLoop, calls=%fused_computation.194 | loop fusion | flops 26542080 | bytes 10616832 | tf_op jit(solution)/shard_map/concatenate | solution.py:21
  125.0 13.4 %collective-permute-start.9 = (bf16[21,24,256]{2,0,1:T(8,128)(2,1)S(1)}, bf16[21,24,256]{2,0,1:T(8,128)(2,1)S(1)}, u32[]{:S(2)}, u32[]{:S(2)}) collective-permute-start(bf16[21,24,256]{2,0,1:T(8,128)(2,1)S(1)} %get-tuple-element.652), channel_id=1, source_target_pairs={{0,4},{4,8},{8,12},{12,16},{16,20},{20,24},{24,28},{28,32},{32,36}... | collective-permute-start | bytes 774152 | tf_op jit(solution)/shard_map/ppermute | solution.py:23
  150.2 11.5 %collective-permute-done.11 = bf16[66,21,256]{2,0,1:T(8,128)(2,1)S(1)} collective-permute-done((bf16[66,21,256]{2,0,1:T(8,128)(2,1)S(1)}, bf16[66,21,256]{2,0,1:T(8,128)(2,1)S(1)}, u32[]{:S(2)}, u32[]{:S(2)}) %collective-permute-start.11) | collective-permute-done | bytes 709664 | tf_op jit(solution)/shard_map/ppermute | solution.py:23
  180.2 9.5 %collective-permute-done.14 = bf16[21,24,512]{2,1,0:T(8,128)(2,1)S(1)} collective-permute-done((bf16[21,24,512]{2,1,0:T(8,128)(2,1)S(1)}, bf16[21,24,512]{2,1,0:T(8,128)(2,1)S(1)}, u32[]{:S(2)}, u32[]{:S(2)}) %collective-permute-start.14) | collective-permute-done | bytes 516128 | tf_op jit(solution)/shard_map/ppermute | solution.py:25
  195.3 21.6 %collective-permute-done.15 = bf16[66,21,512]{2,0,1:T(8,128)(2,1)S(1)} collective-permute-done((bf16[66,21,512]{2,0,1:T(8,128)(2,1)S(1)}, bf16[66,21,512]{2,0,1:T(8,128)(2,1)S(1)}, u32[]{:S(2)}, u32[]{:S(2)}) %collective-permute-start.15) | collective-permute-done | bytes 1419296 | tf_op jit(solution)/shard_map/ppermute | solution.py:23
  227.8 12.3 %collective-permute-start.17 = (bf16[6,24,2048]{2,1,0:T(8,128)(2,1)S(1)}, bf16[6,24,2048]{2,1,0:T(8,128)(2,1)S(1)}, u32[]{:S(2)}, u32[]{:S(2)}) collective-permute-start(bf16[6,24,2048]{2,1,0:T(8,128)(2,1)S(1)} %get-tuple-element.628), channel_id=1, source_target_pairs={{0,4},{4,8},{8,12},{12,16},{16,20},{20,24},{24,28},{28,32},{32,36}... | collective-permute-start | bytes 1769480 | tf_op jit(solution)/shard_map/ppermute | solution.py:23
  283.7 11.3 %all_to_all.46 = bf16[4,6,24,728]{3,2,1,0:T(8,128)(2,1)S(1)} all-to-all(bf16[4,6,24,728]{3,2,1,0:T(8,128)(2,1)S(1)} %copy.139), channel_id=1, replica_groups=mesh['section'=2,'rows'=16,'cols'=4] {'cols'}, dimensions={0} | all-to-all | bytes 1677312 | tf_op jit(solution)/shard_map/all_to_all | solution.py:266
  295.0 78.8 %collective-permute-start.21 = (bf16[6,96,728]{2,1,0:T(8,128)(2,1)S(1)}, bf16[6,96,728]{2,1,0:T(8,128)(2,1)}, u32[]{:S(2)}, u32[]{:S(2)}) collective-permute-start(bf16[6,96,728]{2,1,0:T(8,128)(2,1)S(1)} %bitcast.368), channel_id=1, source_target_pairs={{0,64},{64,0},{1,65},{65,1},{2,66},{66,2},{3,67},{67,3},{4,68},{68... | collective-permute-start | bytes 2515976 | tf_op jit(solution)/shard_map/ppermute | solution.py:33
  373.9 11.3 %collective-permute-done.21 = bf16[6,96,728]{2,1,0:T(8,128)(2,1)} collective-permute-done((bf16[6,96,728]{2,1,0:T(8,128)(2,1)S(1)}, bf16[6,96,728]{2,1,0:T(8,128)(2,1)}, u32[]{:S(2)}, u32[]{:S(2)}) %collective-permute-start.21) | collective-permute-done | bytes 838688 | tf_op jit(solution)/shard_map/ppermute | solution.py:33
  385.6 21.8 %collective-permute-start.22 = (bf16[6,24,2048]{2,1,0:T(8,128)(2,1)S(1)}, bf16[6,24,2048]{2,1,0:T(8,128)(2,1)S(1)}, u32[]{:S(2)}, u32[]{:S(2)}) collective-permute-start(bf16[6,24,2048]{2,1,0:T(8,128)(2,1)S(1)} %get-tuple-element.626), channel_id=1, source_target_pairs={{0,4},{4,8},{8,12},{12,16},{16,20},{20,24},{24,28},{28,32},{32,36}... | collective-permute-start | bytes 1769480 | tf_op jit(solution)/shard_map/ppermute | solution.py:23
  423.5 13.1 %collective-permute-done.24 = bf16[36,6,2048]{2,0,1:T(8,128)(2,1)S(1)} collective-permute-done((bf16[36,6,2048]{2,0,1:T(8,128)(2,1)S(1)}, bf16[36,6,2048]{2,0,1:T(8,128)(2,1)S(1)}, u32[]{:S(2)}, u32[]{:S(2)}) %collective-permute-start.24) | collective-permute-done | bytes 884768 | tf_op jit(solution)/shard_map/ppermute | solution.py:23
  440.7 8.9 %pad_maximum_fusion.6 = bf16[36,36,2048]{2,0,1:T(8,128)(2,1)} fusion(bf16[36,6,2048]{2,0,1:T(8,128)(2,1)S(1)} %collective-permute-done.25, bf16[6,24,2048]{2,0,1:T(8,128)(2,1)S(1)} %copy.144, bf16[24,24,2048]{2,0,1:T(8,128)(2,1)S(1)} %copy.143, bf16[6,24,2048]{2,0,1:T(8,128)(2,1)S(1)} %copy.142, bf16[36,6,2048]{2,0,1:T(8,128)(2,1)S(1)} %collective-permute-done.24), kind=kLoop, calls=%fused_computation.196 | loop fusion | flops 26542080 | bytes 10616832 | tf_op jit(solution)/shard_map/concatenate | solution.py:21
  472.5 9.2 %collective-permute-done.28 = bf16[66,21,256]{2,0,1:T(8,128)(2,1)S(1)} collective-permute-done((bf16[66,21,256]{2,0,1:T(8,128)(2,1)S(1)}, bf16[66,21,256]{2,0,1:T(8,128)(2,1)S(1)}, u32[]{:S(2)}, u32[]{:S(2)}) %collective-permute-start.28) | collective-permute-done | bytes 709664 | tf_op jit(solution)/shard_map/ppermute | solution.py:23
  488.3 8.6 collective-permute-start.30
  513.6 25.3 %collective-permute-done.32 = bf16[66,21,512]{2,0,1:T(8,128)(2,1)S(1)} collective-permute-done((bf16[66,21,512]{2,0,1:T(8,128)(2,1)S(1)}, bf16[66,21,512]{2,0,1:T(8,128)(2,1)S(1)}, u32[]{:S(2)}, u32[]{:S(2)}) %collective-permute-start.32) | collective-permute-done | bytes 1419296 | tf_op jit(solution)/shard_map/ppermute | solution.py:23
  574.7 12.3 %collective-permute-done.36 = bf16[36,6,2048]{2,0,1:T(8,128)(2,1)S(1)} collective-permute-done((bf16[36,6,2048]{2,0,1:T(8,128)(2,1)S(1)}, bf16[36,6,2048]{2,0,1:T(8,128)(2,1)S(1)}, u32[]{:S(2)}, u32[]{:S(2)}) %collective-permute-start.36) | collective-permute-done | bytes 884768 | tf_op jit(solution)/shard_map/ppermute | solution.py:23
  591.2 8.9 %pad_maximum_fusion.7 = bf16[36,36,2048]{2,0,1:T(8,128)(2,1)} fusion(bf16[36,6,2048]{2,0,1:T(8,128)(2,1)S(1)} %collective-permute-done.37, bf16[6,24,2048]{2,0,1:T(8,128)(2,1)S(1)} %copy.158, bf16[24,24,2048]{2,0,1:T(8,128)(2,1)S(1)} %copy.157, bf16[6,24,2048]{2,0,1:T(8,128)(2,1)S(1)} %copy.156, bf16[36,6,2048]{2,0,1:T(8,128)(2,1)S(1)} %collective-permute-done.36), kind=kLoop, calls=%fused_computation.197 | loop fusion | flops 26542080 | bytes 10616832 | tf_op jit(solution)/shard_map/concatenate | solution.py:21
  600.5 11.3 %all_to_all.47 = bf16[4,6,24,728]{3,2,1,0:T(8,128)(2,1)S(1)} all-to-all(bf16[4,6,24,728]{3,2,1,0:T(8,128)(2,1)S(1)} %copy.161), channel_id=1, replica_groups=mesh['section'=2,'rows'=16,'cols'=4] {'cols'}, dimensions={0} | all-to-all | bytes 1677312 | tf_op jit(solution)/shard_map/all_to_all | solution.py:266
  611.9 77.5 %collective-permute-start.38 = (bf16[6,96,728]{2,1,0:T(8,128)(2,1)S(1)}, bf16[6,96,728]{2,1,0:T(8,128)(2,1)}, u32[]{:S(2)}, u32[]{:S(2)}) collective-permute-start(bf16[6,96,728]{2,1,0:T(8,128)(2,1)S(1)} %bitcast.363), channel_id=1, source_target_pairs={{0,64},{64,0},{1,65},{65,1},{2,66},{66,2},{3,67},{67,3},{4,68},{68... | collective-permute-start | bytes 2515976 | tf_op jit(solution)/shard_map/ppermute | solution.py:33
  693.9 10.4 %collective-permute-done.38 = bf16[6,96,728]{2,1,0:T(8,128)(2,1)} collective-permute-done((bf16[6,96,728]{2,1,0:T(8,128)(2,1)S(1)}, bf16[6,96,728]{2,1,0:T(8,128)(2,1)}, u32[]{:S(2)}, u32[]{:S(2)}) %collective-permute-start.38) | collective-permute-done | bytes 838688 | tf_op jit(solution)/shard_map/ppermute | solution.py:33
  711.5 158.1 %all-reduce.5.cloned.1.call-done = (f32[728,728]{1,0:T(8,128)}, f32[2,256,256]{2,1,0:T(8,128)}) async-done(((f32[728,728]{1,0:T(8,128)}, f32[2,256,256]{2,1,0:T(8,128)}), (f32[728,728]{1,0:T(8,128)}, f32[2,256,256]{2,1,0:T(8,128)})) %all-reduce.5.cloned.1.call-update) | async-done | bytes 2644240 | tf_op jit(solution)/shard_map/psum | solution.py:274
  (202 shorter events, 294.7 us)
Async XLA Ops:
  7.2 862.4 %all-reduce.5.cloned.1.call-start = ((), (), s32[]{:S(2)}) async-start(), calls=%async_computation.3 | async-start | bytes 5521408 | tf_op jit(solution)/shard_map/psum | solution.py:274
  8.4 17.4 %collective-permute-start.2 = (bf16[1,96,728]{2,1,0:T(8,128)(2,1)S(1)}, bf16[1,96,728]{2,1,0:T(8,128)(2,1)S(1)}, u32[]{:S(2)}, u32[]{:S(2)}) collective-permute-start(bf16[1,96,728]{2,1,0:T(8,128)(2,1)S(1)} %get-tuple-element.636), channel_id=1, source_target_pairs={{0,1},{1,2},{2,3},{3,4},{4,5},{5,6},{6,7},{7,8},{8,9},{9,10},{10,1... | collective-permute-start | bytes 419336 | tf_op jit(solution)/shard_map/ppermute | solution.py:23
  54.8 22.3 %collective-permute-start.4 = (bf16[6,96,728]{2,1,0:T(8,128)(2,1)S(1)}, bf16[6,96,728]{2,1,0:T(8,128)(2,1)S(1)}, u32[]{:S(2)}, u32[]{:S(2)}) collective-permute-start(bf16[6,96,728]{2,1,0:T(8,128)(2,1)S(1)} %bitcast.367), channel_id=1, source_target_pairs={{0,64},{64,0},{1,65},{65,1},{2,66},{66,2},{3,67},{67,3},{4,68},{68... | collective-permute-start | bytes 2515976 | tf_op jit(solution)/shard_map/ppermute | solution.py:33
  81.4 15.7 %collective-permute-start.6 = (bf16[6,24,2048]{2,1,0:T(8,128)(2,1)S(1)}, bf16[6,24,2048]{2,1,0:T(8,128)(2,1)S(1)}, u32[]{:S(2)}, u32[]{:S(2)}) collective-permute-start(bf16[6,24,2048]{2,1,0:T(8,128)(2,1)S(1)} %get-tuple-element.631), channel_id=1, source_target_pairs={{4,0},{8,4},{12,8},{16,12},{20,16},{24,20},{28,24},{32,28},{36,32}... | collective-permute-start | bytes 1769480 | tf_op jit(solution)/shard_map/ppermute | solution.py:25
  100.4 14.8 %collective-permute-start.8 = (bf16[36,6,2048]{2,0,1:T(8,128)(2,1)S(1)}, bf16[36,6,2048]{2,0,1:T(8,128)(2,1)S(1)}, u32[]{:S(2)}, u32[]{:S(2)}) collective-permute-start(bf16[36,6,2048]{2,0,1:T(8,128)(2,1)S(1)} %get-tuple-element.623), channel_id=1, source_target_pairs={{1,0},{2,1},{3,2},{5,4},{6,5},{7,6},{9,8},{10,9},{11,10},{13,12},{... | collective-permute-start | bytes 2654216 | tf_op jit(solution)/shard_map/ppermute | solution.py:25
  125.0 17.0 %collective-permute-start.9 = (bf16[21,24,256]{2,0,1:T(8,128)(2,1)S(1)}, bf16[21,24,256]{2,0,1:T(8,128)(2,1)S(1)}, u32[]{:S(2)}, u32[]{:S(2)}) collective-permute-start(bf16[21,24,256]{2,0,1:T(8,128)(2,1)S(1)} %get-tuple-element.652), channel_id=1, source_target_pairs={{0,4},{4,8},{8,12},{12,16},{16,20},{20,24},{24,28},{28,32},{32,36}... | collective-permute-start | bytes 774152 | tf_op jit(solution)/shard_map/ppermute | solution.py:23
  148.9 17.1 %collective-permute-start.12 = (bf16[66,21,256]{2,0,1:T(8,128)(2,1)S(1)}, bf16[66,21,256]{2,0,1:T(8,128)(2,1)S(1)}, u32[]{:S(2)}, u32[]{:S(2)}) collective-permute-start(bf16[66,21,256]{2,0,1:T(8,128)(2,1)S(1)} %get-tuple-element.645), channel_id=1, source_target_pairs={{1,0},{2,1},{3,2},{5,4},{6,5},{7,6},{9,8},{10,9},{11,10},{13,12},{... | collective-permute-start | bytes 2128904 | tf_op jit(solution)/shard_map/ppermute | solution.py:25
  174.0 15.6 %collective-permute-start.14 = (bf16[21,24,512]{2,1,0:T(8,128)(2,1)S(1)}, bf16[21,24,512]{2,1,0:T(8,128)(2,1)S(1)}, u32[]{:S(2)}, u32[]{:S(2)}) collective-permute-start(bf16[21,24,512]{2,1,0:T(8,128)(2,1)S(1)} %get-tuple-element.649), channel_id=1, source_target_pairs={{4,0},{8,4},{12,8},{16,12},{20,16},{24,20},{28,24},{32,28},{36,32}... | collective-permute-start | bytes 1548296 | tf_op jit(solution)/shard_map/ppermute | solution.py:25
  190.6 26.3 %collective-permute-start.15 = (bf16[66,21,512]{2,0,1:T(8,128)(2,1)S(1)}, bf16[66,21,512]{2,0,1:T(8,128)(2,1)S(1)}, u32[]{:S(2)}, u32[]{:S(2)}) collective-permute-start(bf16[66,21,512]{2,0,1:T(8,128)(2,1)S(1)} %get-tuple-element.634), channel_id=1, source_target_pairs={{0,1},{1,2},{2,3},{4,5},{5,6},{6,7},{8,9},{9,10},{10,11},{12,13},{... | collective-permute-start | bytes 4257800 | tf_op jit(solution)/shard_map/ppermute | solution.py:23
  194.0 27.1 %collective-permute-start.16 = (bf16[66,21,512]{2,0,1:T(8,128)(2,1)S(1)}, bf16[66,21,512]{2,0,1:T(8,128)(2,1)S(1)}, u32[]{:S(2)}, u32[]{:S(2)}) collective-permute-start(bf16[66,21,512]{2,0,1:T(8,128)(2,1)S(1)} %get-tuple-element.635), channel_id=1, source_target_pairs={{1,0},{2,1},{3,2},{5,4},{6,5},{7,6},{9,8},{10,9},{11,10},{13,12},{... | collective-permute-start | bytes 4257800 | tf_op jit(solution)/shard_map/ppermute | solution.py:25
  227.8 19.1 %collective-permute-start.17 = (bf16[6,24,2048]{2,1,0:T(8,128)(2,1)S(1)}, bf16[6,24,2048]{2,1,0:T(8,128)(2,1)S(1)}, u32[]{:S(2)}, u32[]{:S(2)}) collective-permute-start(bf16[6,24,2048]{2,1,0:T(8,128)(2,1)S(1)} %get-tuple-element.628), channel_id=1, source_target_pairs={{0,4},{4,8},{8,12},{12,16},{16,20},{20,24},{24,28},{28,32},{32,36}... | collective-permute-start | bytes 1769480 | tf_op jit(solution)/shard_map/ppermute | solution.py:23
  240.1 15.6 %collective-permute-start.18 = (bf16[6,24,2048]{2,1,0:T(8,128)(2,1)S(1)}, bf16[6,24,2048]{2,1,0:T(8,128)(2,1)S(1)}, u32[]{:S(2)}, u32[]{:S(2)}) collective-permute-start(bf16[6,24,2048]{2,1,0:T(8,128)(2,1)S(1)} %get-tuple-element.629), channel_id=1, source_target_pairs={{4,0},{8,4},{12,8},{16,12},{20,16},{24,20},{28,24},{32,28},{36,32}... | collective-permute-start | bytes 1769480 | tf_op jit(solution)/shard_map/ppermute | solution.py:25
  260.9 15.1 %collective-permute-start.20 = (bf16[36,6,2048]{2,0,1:T(8,128)(2,1)}, bf16[36,6,2048]{2,0,1:T(8,128)(2,1)}, u32[]{:S(2)}, u32[]{:S(2)}) collective-permute-start(bf16[36,6,2048]{2,0,1:T(8,128)(2,1)} %get-tuple-element.621), channel_id=1, source_target_pairs={{1,0},{2,1},{3,2},{5,4},{6,5},{7,6},{9,8},{10,9},{11,10},{13,12},{... | collective-permute-start | bytes 2654216 | tf_op jit(solution)/shard_map/ppermute | solution.py:25
  295.0 90.1 %collective-permute-start.21 = (bf16[6,96,728]{2,1,0:T(8,128)(2,1)S(1)}, bf16[6,96,728]{2,1,0:T(8,128)(2,1)}, u32[]{:S(2)}, u32[]{:S(2)}) collective-permute-start(bf16[6,96,728]{2,1,0:T(8,128)(2,1)S(1)} %bitcast.368), channel_id=1, source_target_pairs={{0,64},{64,0},{1,65},{65,1},{2,66},{66,2},{3,67},{67,3},{4,68},{68... | collective-permute-start | bytes 2515976 | tf_op jit(solution)/shard_map/ppermute | solution.py:33
  385.6 28.6 %collective-permute-start.22 = (bf16[6,24,2048]{2,1,0:T(8,128)(2,1)S(1)}, bf16[6,24,2048]{2,1,0:T(8,128)(2,1)S(1)}, u32[]{:S(2)}, u32[]{:S(2)}) collective-permute-start(bf16[6,24,2048]{2,1,0:T(8,128)(2,1)S(1)} %get-tuple-element.626), channel_id=1, source_target_pairs={{0,4},{4,8},{8,12},{12,16},{16,20},{20,24},{24,28},{28,32},{32,36}... | collective-permute-start | bytes 1769480 | tf_op jit(solution)/shard_map/ppermute | solution.py:23
  419.7 16.9 %collective-permute-start.24 = (bf16[36,6,2048]{2,0,1:T(8,128)(2,1)S(1)}, bf16[36,6,2048]{2,0,1:T(8,128)(2,1)S(1)}, u32[]{:S(2)}, u32[]{:S(2)}) collective-permute-start(bf16[36,6,2048]{2,0,1:T(8,128)(2,1)S(1)} %get-tuple-element.618), channel_id=1, source_target_pairs={{0,1},{1,2},{2,3},{4,5},{5,6},{6,7},{8,9},{9,10},{10,11},{12,13},{... | collective-permute-start | bytes 2654216 | tf_op jit(solution)/shard_map/ppermute | solution.py:23
  422.2 18.5 %collective-permute-start.25 = (bf16[36,6,2048]{2,0,1:T(8,128)(2,1)S(1)}, bf16[36,6,2048]{2,0,1:T(8,128)(2,1)S(1)}, u32[]{:S(2)}, u32[]{:S(2)}) collective-permute-start(bf16[36,6,2048]{2,0,1:T(8,128)(2,1)S(1)} %get-tuple-element.619), channel_id=1, source_target_pairs={{1,0},{2,1},{3,2},{5,4},{6,5},{7,6},{9,8},{10,9},{11,10},{13,12},{... | collective-permute-start | bytes 2654216 | tf_op jit(solution)/shard_map/ppermute | solution.py:25
  471.2 14.7 %collective-permute-start.29 = (bf16[66,21,256]{2,0,1:T(8,128)(2,1)S(1)}, bf16[66,21,256]{2,0,1:T(8,128)(2,1)S(1)}, u32[]{:S(2)}, u32[]{:S(2)}) collective-permute-start(bf16[66,21,256]{2,0,1:T(8,128)(2,1)S(1)} %get-tuple-element.643), channel_id=1, source_target_pairs={{1,0},{2,1},{3,2},{5,4},{6,5},{7,6},{9,8},{10,9},{11,10},{13,12},{... | collective-permute-start | bytes 2128904 | tf_op jit(solution)/shard_map/ppermute | solution.py:25
  509.1 29.8 %collective-permute-start.32 = (bf16[66,21,512]{2,0,1:T(8,128)(2,1)S(1)}, bf16[66,21,512]{2,0,1:T(8,128)(2,1)S(1)}, u32[]{:S(2)}, u32[]{:S(2)}) collective-permute-start(bf16[66,21,512]{2,0,1:T(8,128)(2,1)S(1)} %get-tuple-element.632), channel_id=1, source_target_pairs={{0,1},{1,2},{2,3},{4,5},{5,6},{6,7},{8,9},{9,10},{10,11},{12,13},{... | collective-permute-start | bytes 4257800 | tf_op jit(solution)/shard_map/ppermute | solution.py:23
  512.3 30.8 %collective-permute-start.33 = (bf16[66,21,512]{2,0,1:T(8,128)(2,1)S(1)}, bf16[66,21,512]{2,0,1:T(8,128)(2,1)S(1)}, u32[]{:S(2)}, u32[]{:S(2)}) collective-permute-start(bf16[66,21,512]{2,0,1:T(8,128)(2,1)S(1)} %get-tuple-element.633), channel_id=1, source_target_pairs={{1,0},{2,1},{3,2},{5,4},{6,5},{7,6},{9,8},{10,9},{11,10},{13,12},{... | collective-permute-start | bytes 4257800 | tf_op jit(solution)/shard_map/ppermute | solution.py:25
  549.7 15.0 %collective-permute-start.34 = (bf16[6,24,2048]{2,1,0:T(8,128)(2,1)S(1)}, bf16[6,24,2048]{2,1,0:T(8,128)(2,1)S(1)}, u32[]{:S(2)}, u32[]{:S(2)}) collective-permute-start(bf16[6,24,2048]{2,1,0:T(8,128)(2,1)S(1)} %get-tuple-element.624), channel_id=1, source_target_pairs={{0,4},{4,8},{8,12},{12,16},{16,20},{20,24},{24,28},{28,32},{32,36}... | collective-permute-start | bytes 1769480 | tf_op jit(solution)/shard_map/ppermute | solution.py:23
  571.0 16.1 %collective-permute-start.36 = (bf16[36,6,2048]{2,0,1:T(8,128)(2,1)S(1)}, bf16[36,6,2048]{2,0,1:T(8,128)(2,1)S(1)}, u32[]{:S(2)}, u32[]{:S(2)}) collective-permute-start(bf16[36,6,2048]{2,0,1:T(8,128)(2,1)S(1)} %get-tuple-element.616), channel_id=1, source_target_pairs={{0,1},{1,2},{2,3},{4,5},{5,6},{6,7},{8,9},{9,10},{10,11},{12,13},{... | collective-permute-start | bytes 2654216 | tf_op jit(solution)/shard_map/ppermute | solution.py:23
  573.4 17.8 %collective-permute-start.37 = (bf16[36,6,2048]{2,0,1:T(8,128)(2,1)S(1)}, bf16[36,6,2048]{2,0,1:T(8,128)(2,1)S(1)}, u32[]{:S(2)}, u32[]{:S(2)}) collective-permute-start(bf16[36,6,2048]{2,0,1:T(8,128)(2,1)S(1)} %get-tuple-element.617), channel_id=1, source_target_pairs={{1,0},{2,1},{3,2},{5,4},{6,5},{7,6},{9,8},{10,9},{11,10},{13,12},{... | collective-permute-start | bytes 2654216 | tf_op jit(solution)/shard_map/ppermute | solution.py:25
  611.9 92.5 %collective-permute-start.38 = (bf16[6,96,728]{2,1,0:T(8,128)(2,1)S(1)}, bf16[6,96,728]{2,1,0:T(8,128)(2,1)}, u32[]{:S(2)}, u32[]{:S(2)}) collective-permute-start(bf16[6,96,728]{2,1,0:T(8,128)(2,1)S(1)} %bitcast.363), channel_id=1, source_target_pairs={{0,64},{64,0},{1,65},{65,1},{2,66},{66,2},{3,67},{67,3},{4,68},{68... | collective-permute-start | bytes 2515976 | tf_op jit(solution)/shard_map/ppermute | solution.py:33
  (35 other events, 390.8 us)
Sparse Core Ops, SparseCore 0:
  711.7 157.9 all-reduce.4
where the time goes:
time: 890 us; the launch traced here: 881 us
  waiting for transfers between devices  417 us (47%)
  starting transfers between devices  300 us (34%)
  other arithmetic  66.2 us (7%)
  blocking collectives  42.7 us (5%)
  local copies, waits for them, and re-layouts  27.7 us (3%)
  between operations  15.3 us (2%)
  matrix products  10.4 us (1%)
    psum x1, waiting for transfers between devices, local(): lax.psum((grad_mid, grad_later), ('section', 'rows', 'cols'))  158 us
    ppermute x3, starting transfers between devices, from_partner(): lax.ppermute(value, axis, [(i, i ^ 1 << distance) for i in range(lax.axis...  156 us
    ppermute x18, waiting for transfers between devices, with_halo(): lax.ppermute(tail, axis, [(i, (i + 1) % count) for i in range(ends)])  129 us
    ppermute x18, starting transfers between devices, with_halo(): lax.ppermute(tail, axis, [(i, (i + 1) % count) for i in range(ends)])  107 us
    ppermute x18, waiting for transfers between devices, with_halo(): lax.ppermute(head, axis, [((i + 1) % count, i) for i in range(ends)])  86.4 us
    concatenate x13, other arithmetic, with_halo(): jnp.concatenate([lax.ppermute(tail, axis, [(i, (i + 1) % count) for i in...  49 us
    ppermute x3, waiting for transfers between devices, from_partner(): lax.ppermute(value, axis, [(i, i ^ 1 << distance) for i in range(lax.axis...  44 us
    all_to_all x3, blocking collectives, local(): lax.all_to_all(message, 'cols', split_axis=0, concat_axis=2, tiled=True)  42.7 us
  transfers between devices with their start and end apart: 40, of which 37 were waited for; matrix products, arithmetic and copies ran while one was open for 2% of the time, Pallas kernels for 0%

commit v1 on v0

--- a/solution.py
+++ b/solution.py
@@ -271,7 +271,7 @@
             grad_mid = grad_mid + section_only(
                 leading, mid_gradient, saved_convs[moment - 1], received
             )
-    grad_mid, grad_later = lax.psum((grad_mid, grad_later), ("section", "rows", "cols"))
+    grad_mid, grad_later = lax.psum(lax.psum((grad_mid, grad_later), ("rows", "cols")), "section")
     return (grad_mid, grad_later)
 
 

time: 890 us -> 1370 us (1.54)
  waiting for transfers between devices: 417 us -> 899 us
    psum x1 -> x2, waiting for transfers between devices: 158 us -> 640 us  [the longest x1 556 us: local(): lax.psum((grad_mid, grad_later), ('rows', 'cols'))]
  transfers between devices with their start and end apart: 40 -> 41, of which waited for: 37 -> 38; matrix products, arithmetic and copies ran while one was open for 2% -> 2% of each run, Pallas kernels for 0% -> 0%
where the time goes in v1:
time: 1370 us; the launch traced here: 1360 us
  waiting for transfers between devices  899 us (66%)
  starting transfers between devices  297 us (22%)
  other arithmetic  66.1 us (5%)
  blocking collectives  42.7 us (3%)
  local copies, waits for them, and re-layouts  27.7 us (2%)
  between operations  15.3 us (1%)
    psum x1, waiting for transfers between devices, local(): lax.psum((grad_mid, grad_later), ('rows', 'cols'))  556 us
    ppermute x3, starting transfers between devices, from_partner(): lax.ppermute(value, axis, [(i, i ^ 1 << distance) for i in range(lax.axis...  153 us
    ppermute x18, waiting for transfers between devices, with_halo(): lax.ppermute(tail, axis, [(i, (i + 1) % count) for i in range(ends)])  129 us
    ppermute x18, starting transfers between devices, with_halo(): lax.ppermute(tail, axis, [(i, (i + 1) % count) for i in range(ends)])  108 us
    ppermute x18, waiting for transfers between devices, with_halo(): lax.ppermute(head, axis, [((i + 1) % count, i) for i in range(ends)])  86.5 us
    psum x1, waiting for transfers between devices, local(): lax.psum(lax.psum((grad_mid, grad_later), ('rows', 'cols')), 'section')  84.2 us
    concatenate x13, other arithmetic, with_halo(): jnp.concatenate([lax.ppermute(tail, axis, [(i, (i + 1) % count) for i in...  48.8 us
    ppermute x3, waiting for transfers between devices, from_partner(): lax.ppermute(value, axis, [(i, i ^ 1 << distance) for i in range(lax.axis...  44 us
  transfers between devices with their start and end apart: 41, of which 38 were waited for; matrix products, arithmetic and copies ran while one was open for 2% of the time, Pallas kernels for 0%

profile of v1, /device:TPU:1, one launch (start us, length us, event | category | flops | bytes accessed | tf_op | source)
XLA Modules:
  0.0 1359.7 jit_solution(5489160827162097863)
XLA Ops:
  34.7 20.1 %all_to_all.45 = bf16[4,6,24,728]{3,2,1,0:T(8,128)(2,1)S(1)} all-to-all(bf16[4,6,24,728]{3,2,1,0:T(8,128)(2,1)S(1)} %copy.117), channel_id=1, replica_groups=mesh['section'=2,'rows'=16,'cols'=4] {'cols'}, dimensions={0} | all-to-all | bytes 1677312 | tf_op jit(solution)/shard_map/all_to_all | solution.py:266
  55.0 22.2 %collective-permute-done.4 = bf16[6,96,728]{2,1,0:T(8,128)(2,1)S(1)} collective-permute-done((bf16[6,96,728]{2,1,0:T(8,128)(2,1)S(1)}, bf16[6,96,728]{2,1,0:T(8,128)(2,1)S(1)}, u32[]{:S(2)}, u32[]{:S(2)}) %collective-permute-start.4) | collective-permute-done | bytes 838688 | tf_op jit(solution)/shard_map/ppermute | solution.py:33
  102.0 9.4 collective-permute-done.7
  115.3 8.9 pad_maximum_fusion.4
  125.1 13.4 collective-permute-start.9
  150.3 11.5 collective-permute-done.11
  180.2 9.5 collective-permute-done.14
  195.4 21.6 %collective-permute-done.15 = bf16[66,21,512]{2,0,1:T(8,128)(2,1)S(1)} collective-permute-done((bf16[66,21,512]{2,0,1:T(8,128)(2,1)S(1)}, bf16[66,21,512]{2,0,1:T(8,128)(2,1)S(1)}, u32[]{:S(2)}, u32[]{:S(2)}) %collective-permute-start.15) | collective-permute-done | bytes 1419296 | tf_op jit(solution)/shard_map/ppermute | solution.py:23
  227.7 12.3 collective-permute-start.17
  283.7 11.3 all_to_all.46
  295.0 77.3 %collective-permute-start.21 = (bf16[6,96,728]{2,1,0:T(8,128)(2,1)S(1)}, bf16[6,96,728]{2,1,0:T(8,128)(2,1)}, u32[]{:S(2)}, u32[]{:S(2)}) collective-permute-start(bf16[6,96,728]{2,1,0:T(8,128)(2,1)S(1)} %bitcast.368), channel_id=1, source_target_pairs={{0,64},{64,0},{1,65},{65,1},{2,66},{66,2},{3,67},{67,3},{4,68},{68... | collective-permute-start | bytes 2515976 | tf_op jit(solution)/shard_map/ppermute | solution.py:33
  372.2 11.3 collective-permute-done.21
  384.0 21.8 %collective-permute-start.22 = (bf16[6,24,2048]{2,1,0:T(8,128)(2,1)S(1)}, bf16[6,24,2048]{2,1,0:T(8,128)(2,1)S(1)}, u32[]{:S(2)}, u32[]{:S(2)}) collective-permute-start(bf16[6,24,2048]{2,1,0:T(8,128)(2,1)S(1)} %get-tuple-element.628), channel_id=1, source_target_pairs={{0,4},{4,8},{8,12},{12,16},{16,20},{20,24},{24,28},{28,32},{32,36}... | collective-permute-start | bytes 1769480 | tf_op jit(solution)/shard_map/ppermute | solution.py:23
  421.9 13.1 collective-permute-done.24
  439.1 8.9 pad_maximum_fusion.6
  471.0 9.2 collective-permute-done.28
  512.2 25.2 %collective-permute-done.32 = bf16[66,21,512]{2,0,1:T(8,128)(2,1)S(1)} collective-permute-done((bf16[66,21,512]{2,0,1:T(8,128)(2,1)S(1)}, bf16[66,21,512]{2,0,1:T(8,128)(2,1)S(1)}, u32[]{:S(2)}, u32[]{:S(2)}) %collective-permute-start.32) | collective-permute-done | bytes 1419296 | tf_op jit(solution)/shard_map/ppermute | solution.py:23
  573.3 12.3 collective-permute-done.36
  589.8 8.9 pad_maximum_fusion.7
  599.1 11.3 all_to_all.47
  610.4 75.9 %collective-permute-start.38 = (bf16[6,96,728]{2,1,0:T(8,128)(2,1)S(1)}, bf16[6,96,728]{2,1,0:T(8,128)(2,1)}, u32[]{:S(2)}, u32[]{:S(2)}) collective-permute-start(bf16[6,96,728]{2,1,0:T(8,128)(2,1)S(1)} %bitcast.363), channel_id=1, source_target_pairs={{0,64},{64,0},{1,65},{65,1},{2,66},{66,2},{3,67},{67,3},{4,68},{68... | collective-permute-start | bytes 2515976 | tf_op jit(solution)/shard_map/ppermute | solution.py:33
  690.9 10.4 collective-permute-done.38
  708.6 555.7 %all-reduce.7.cloned.1.call-done = (f32[728,728]{1,0:T(8,128)}, f32[2,256,256]{2,1,0:T(8,128)}) async-done(((f32[728,728]{1,0:T(8,128)}, f32[2,256,256]{2,1,0:T(8,128)}), (f32[728,728]{1,0:T(8,128)}, f32[2,256,256]{2,1,0:T(8,128)})) %all-reduce.7.cloned.1.call-update) | async-done | bytes 2644240 | tf_op jit(solution)/shard_map/psum | solution.py:274
  1264.3 84.2 %all-reduce.9.cloned.1.call-done = (f32[728,728]{1,0:T(8,128)}, f32[2,256,256]{2,1,0:T(8,128)}) async-done(((f32[728,728]{1,0:T(8,128)}, f32[2,256,256]{2,1,0:T(8,128)}), (f32[728,728]{1,0:T(8,128)}, f32[2,256,256]{2,1,0:T(8,128)})) %all-reduce.9.cloned.1.call-update) | async-done | bytes 2644240 | tf_op jit(solution)/shard_map/psum | solution.py:274
  (205 shorter events, 303.6 us)
Async XLA Ops:
  7.2 1257.1 %all-reduce.7.cloned.1.call-start = ((), (), s32[]{:S(2)}) async-start(), calls=%async_computation.3 | async-start | bytes 5521408 | tf_op jit(solution)/shard_map/psum | solution.py:274
  8.4 17.4 %collective-permute-start.2 = (bf16[1,96,728]{2,1,0:T(8,128)(2,1)S(1)}, bf16[1,96,728]{2,1,0:T(8,128)(2,1)S(1)}, u32[]{:S(2)}, u32[]{:S(2)}) collective-permute-start(bf16[1,96,728]{2,1,0:T(8,128)(2,1)S(1)} %get-tuple-element.638), channel_id=1, source_target_pairs={{0,1},{1,2},{2,3},{3,4},{4,5},{5,6},{6,7},{7,8},{8,9},{9,10},{10,1... | collective-permute-start | bytes 419336 | tf_op jit(solution)/shard_map/ppermute | solution.py:23
  54.9 22.3 %collective-permute-start.4 = (bf16[6,96,728]{2,1,0:T(8,128)(2,1)S(1)}, bf16[6,96,728]{2,1,0:T(8,128)(2,1)S(1)}, u32[]{:S(2)}, u32[]{:S(2)}) collective-permute-start(bf16[6,96,728]{2,1,0:T(8,128)(2,1)S(1)} %bitcast.367), channel_id=1, source_target_pairs={{0,64},{64,0},{1,65},{65,1},{2,66},{66,2},{3,67},{67,3},{4,68},{68... | collective-permute-start | bytes 2515976 | tf_op jit(solution)/shard_map/ppermute | solution.py:33
  81.4 15.7 %collective-permute-start.6 = (bf16[6,24,2048]{2,1,0:T(8,128)(2,1)S(1)}, bf16[6,24,2048]{2,1,0:T(8,128)(2,1)S(1)}, u32[]{:S(2)}, u32[]{:S(2)}) collective-permute-start(bf16[6,24,2048]{2,1,0:T(8,128)(2,1)S(1)} %get-tuple-element.633), channel_id=1, source_target_pairs={{4,0},{8,4},{12,8},{16,12},{20,16},{24,20},{28,24},{32,28},{36,32}... | collective-permute-start | bytes 1769480 | tf_op jit(solution)/shard_map/ppermute | solution.py:25
  100.5 14.8 %collective-permute-start.8 = (bf16[36,6,2048]{2,0,1:T(8,128)(2,1)S(1)}, bf16[36,6,2048]{2,0,1:T(8,128)(2,1)S(1)}, u32[]{:S(2)}, u32[]{:S(2)}) collective-permute-start(bf16[36,6,2048]{2,0,1:T(8,128)(2,1)S(1)} %get-tuple-element.625), channel_id=1, source_target_pairs={{1,0},{2,1},{3,2},{5,4},{6,5},{7,6},{9,8},{10,9},{11,10},{13,12},{... | collective-permute-start | bytes 2654216 | tf_op jit(solution)/shard_map/ppermute | solution.py:25
  125.1 17.0 %collective-permute-start.9 = (bf16[21,24,256]{2,0,1:T(8,128)(2,1)S(1)}, bf16[21,24,256]{2,0,1:T(8,128)(2,1)S(1)}, u32[]{:S(2)}, u32[]{:S(2)}) collective-permute-start(bf16[21,24,256]{2,0,1:T(8,128)(2,1)S(1)} %get-tuple-element.654), channel_id=1, source_target_pairs={{0,4},{4,8},{8,12},{12,16},{16,20},{20,24},{24,28},{28,32},{32,36}... | collective-permute-start | bytes 774152 | tf_op jit(solution)/shard_map/ppermute | solution.py:23
  149.0 17.1 %collective-permute-start.12 = (bf16[66,21,256]{2,0,1:T(8,128)(2,1)S(1)}, bf16[66,21,256]{2,0,1:T(8,128)(2,1)S(1)}, u32[]{:S(2)}, u32[]{:S(2)}) collective-permute-start(bf16[66,21,256]{2,0,1:T(8,128)(2,1)S(1)} %get-tuple-element.647), channel_id=1, source_target_pairs={{1,0},{2,1},{3,2},{5,4},{6,5},{7,6},{9,8},{10,9},{11,10},{13,12},{... | collective-permute-start | bytes 2128904 | tf_op jit(solution)/shard_map/ppermute | solution.py:25
  174.0 15.6 %collective-permute-start.14 = (bf16[21,24,512]{2,1,0:T(8,128)(2,1)S(1)}, bf16[21,24,512]{2,1,0:T(8,128)(2,1)S(1)}, u32[]{:S(2)}, u32[]{:S(2)}) collective-permute-start(bf16[21,24,512]{2,1,0:T(8,128)(2,1)S(1)} %get-tuple-element.651), channel_id=1, source_target_pairs={{4,0},{8,4},{12,8},{16,12},{20,16},{24,20},{28,24},{32,28},{36,32}... | collective-permute-start | bytes 1548296 | tf_op jit(solution)/shard_map/ppermute | solution.py:25
  190.7 26.3 %collective-permute-start.15 = (bf16[66,21,512]{2,0,1:T(8,128)(2,1)S(1)}, bf16[66,21,512]{2,0,1:T(8,128)(2,1)S(1)}, u32[]{:S(2)}, u32[]{:S(2)}) collective-permute-start(bf16[66,21,512]{2,0,1:T(8,128)(2,1)S(1)} %get-tuple-element.636), channel_id=1, source_target_pairs={{0,1},{1,2},{2,3},{4,5},{5,6},{6,7},{8,9},{9,10},{10,11},{12,13},{... | collective-permute-start | bytes 4257800 | tf_op jit(solution)/shard_map/ppermute | solution.py:23
  194.1 27.1 %collective-permute-start.16 = (bf16[66,21,512]{2,0,1:T(8,128)(2,1)S(1)}, bf16[66,21,512]{2,0,1:T(8,128)(2,1)S(1)}, u32[]{:S(2)}, u32[]{:S(2)}) collective-permute-start(bf16[66,21,512]{2,0,1:T(8,128)(2,1)S(1)} %get-tuple-element.637), channel_id=1, source_target_pairs={{1,0},{2,1},{3,2},{5,4},{6,5},{7,6},{9,8},{10,9},{11,10},{13,12},{... | collective-permute-start | bytes 4257800 | tf_op jit(solution)/shard_map/ppermute | solution.py:25
  227.7 19.1 %collective-permute-start.17 = (bf16[6,24,2048]{2,1,0:T(8,128)(2,1)S(1)}, bf16[6,24,2048]{2,1,0:T(8,128)(2,1)S(1)}, u32[]{:S(2)}, u32[]{:S(2)}) collective-permute-start(bf16[6,24,2048]{2,1,0:T(8,128)(2,1)S(1)} %get-tuple-element.630), channel_id=1, source_target_pairs={{0,4},{4,8},{8,12},{12,16},{16,20},{20,24},{24,28},{28,32},{32,36}... | collective-permute-start | bytes 1769480 | tf_op jit(solution)/shard_map/ppermute | solution.py:23
  240.1 15.6 %collective-permute-start.18 = (bf16[6,24,2048]{2,1,0:T(8,128)(2,1)S(1)}, bf16[6,24,2048]{2,1,0:T(8,128)(2,1)S(1)}, u32[]{:S(2)}, u32[]{:S(2)}) collective-permute-start(bf16[6,24,2048]{2,1,0:T(8,128)(2,1)S(1)} %get-tuple-element.631), channel_id=1, source_target_pairs={{4,0},{8,4},{12,8},{16,12},{20,16},{24,20},{28,24},{32,28},{36,32}... | collective-permute-start | bytes 1769480 | tf_op jit(solution)/shard_map/ppermute | solution.py:25
  260.9 15.1 %collective-permute-start.20 = (bf16[36,6,2048]{2,0,1:T(8,128)(2,1)}, bf16[36,6,2048]{2,0,1:T(8,128)(2,1)}, u32[]{:S(2)}, u32[]{:S(2)}) collective-permute-start(bf16[36,6,2048]{2,0,1:T(8,128)(2,1)} %get-tuple-element.623), channel_id=1, source_target_pairs={{1,0},{2,1},{3,2},{5,4},{6,5},{7,6},{9,8},{10,9},{11,10},{13,12},{... | collective-permute-start | bytes 2654216 | tf_op jit(solution)/shard_map/ppermute | solution.py:25
  295.0 88.6 %collective-permute-start.21 = (bf16[6,96,728]{2,1,0:T(8,128)(2,1)S(1)}, bf16[6,96,728]{2,1,0:T(8,128)(2,1)}, u32[]{:S(2)}, u32[]{:S(2)}) collective-permute-start(bf16[6,96,728]{2,1,0:T(8,128)(2,1)S(1)} %bitcast.368), channel_id=1, source_target_pairs={{0,64},{64,0},{1,65},{65,1},{2,66},{66,2},{3,67},{67,3},{4,68},{68... | collective-permute-start | bytes 2515976 | tf_op jit(solution)/shard_map/ppermute | solution.py:33
  384.0 28.6 %collective-permute-start.22 = (bf16[6,24,2048]{2,1,0:T(8,128)(2,1)S(1)}, bf16[6,24,2048]{2,1,0:T(8,128)(2,1)S(1)}, u32[]{:S(2)}, u32[]{:S(2)}) collective-permute-start(bf16[6,24,2048]{2,1,0:T(8,128)(2,1)S(1)} %get-tuple-element.628), channel_id=1, source_target_pairs={{0,4},{4,8},{8,12},{12,16},{16,20},{20,24},{24,28},{28,32},{32,36}... | collective-permute-start | bytes 1769480 | tf_op jit(solution)/shard_map/ppermute | solution.py:23
  418.0 16.9 %collective-permute-start.24 = (bf16[36,6,2048]{2,0,1:T(8,128)(2,1)S(1)}, bf16[36,6,2048]{2,0,1:T(8,128)(2,1)S(1)}, u32[]{:S(2)}, u32[]{:S(2)}) collective-permute-start(bf16[36,6,2048]{2,0,1:T(8,128)(2,1)S(1)} %get-tuple-element.620), channel_id=1, source_target_pairs={{0,1},{1,2},{2,3},{4,5},{5,6},{6,7},{8,9},{9,10},{10,11},{12,13},{... | collective-permute-start | bytes 2654216 | tf_op jit(solution)/shard_map/ppermute | solution.py:23
  420.6 18.5 %collective-permute-start.25 = (bf16[36,6,2048]{2,0,1:T(8,128)(2,1)S(1)}, bf16[36,6,2048]{2,0,1:T(8,128)(2,1)S(1)}, u32[]{:S(2)}, u32[]{:S(2)}) collective-permute-start(bf16[36,6,2048]{2,0,1:T(8,128)(2,1)S(1)} %get-tuple-element.621), channel_id=1, source_target_pairs={{1,0},{2,1},{3,2},{5,4},{6,5},{7,6},{9,8},{10,9},{11,10},{13,12},{... | collective-permute-start | bytes 2654216 | tf_op jit(solution)/shard_map/ppermute | solution.py:25
  507.7 29.7 %collective-permute-start.32 = (bf16[66,21,512]{2,0,1:T(8,128)(2,1)S(1)}, bf16[66,21,512]{2,0,1:T(8,128)(2,1)S(1)}, u32[]{:S(2)}, u32[]{:S(2)}) collective-permute-start(bf16[66,21,512]{2,0,1:T(8,128)(2,1)S(1)} %get-tuple-element.634), channel_id=1, source_target_pairs={{0,1},{1,2},{2,3},{4,5},{5,6},{6,7},{8,9},{9,10},{10,11},{12,13},{... | collective-permute-start | bytes 4257800 | tf_op jit(solution)/shard_map/ppermute | solution.py:23
  510.9 30.7 %collective-permute-start.33 = (bf16[66,21,512]{2,0,1:T(8,128)(2,1)S(1)}, bf16[66,21,512]{2,0,1:T(8,128)(2,1)S(1)}, u32[]{:S(2)}, u32[]{:S(2)}) collective-permute-start(bf16[66,21,512]{2,0,1:T(8,128)(2,1)S(1)} %get-tuple-element.635), channel_id=1, source_target_pairs={{1,0},{2,1},{3,2},{5,4},{6,5},{7,6},{9,8},{10,9},{11,10},{13,12},{... | collective-permute-start | bytes 4257800 | tf_op jit(solution)/shard_map/ppermute | solution.py:25
  548.2 15.1 %collective-permute-start.34 = (bf16[6,24,2048]{2,1,0:T(8,128)(2,1)S(1)}, bf16[6,24,2048]{2,1,0:T(8,128)(2,1)S(1)}, u32[]{:S(2)}, u32[]{:S(2)}) collective-permute-start(bf16[6,24,2048]{2,1,0:T(8,128)(2,1)S(1)} %get-tuple-element.626), channel_id=1, source_target_pairs={{0,4},{4,8},{8,12},{12,16},{16,20},{20,24},{24,28},{28,32},{32,36}... | collective-permute-start | bytes 1769480 | tf_op jit(solution)/shard_map/ppermute | solution.py:23
  569.5 16.1 %collective-permute-start.36 = (bf16[36,6,2048]{2,0,1:T(8,128)(2,1)S(1)}, bf16[36,6,2048]{2,0,1:T(8,128)(2,1)S(1)}, u32[]{:S(2)}, u32[]{:S(2)}) collective-permute-start(bf16[36,6,2048]{2,0,1:T(8,128)(2,1)S(1)} %get-tuple-element.618), channel_id=1, source_target_pairs={{0,1},{1,2},{2,3},{4,5},{5,6},{6,7},{8,9},{9,10},{10,11},{12,13},{... | collective-permute-start | bytes 2654216 | tf_op jit(solution)/shard_map/ppermute | solution.py:23
  572.0 17.8 %collective-permute-start.37 = (bf16[36,6,2048]{2,0,1:T(8,128)(2,1)S(1)}, bf16[36,6,2048]{2,0,1:T(8,128)(2,1)S(1)}, u32[]{:S(2)}, u32[]{:S(2)}) collective-permute-start(bf16[36,6,2048]{2,0,1:T(8,128)(2,1)S(1)} %get-tuple-element.619), channel_id=1, source_target_pairs={{1,0},{2,1},{3,2},{5,4},{6,5},{7,6},{9,8},{10,9},{11,10},{13,12},{... | collective-permute-start | bytes 2654216 | tf_op jit(solution)/shard_map/ppermute | solution.py:25
  610.4 90.9 %collective-permute-start.38 = (bf16[6,96,728]{2,1,0:T(8,128)(2,1)S(1)}, bf16[6,96,728]{2,1,0:T(8,128)(2,1)}, u32[]{:S(2)}, u32[]{:S(2)}) collective-permute-start(bf16[6,96,728]{2,1,0:T(8,128)(2,1)S(1)} %bitcast.363), channel_id=1, source_target_pairs={{0,64},{64,0},{1,65},{65,1},{2,66},{66,2},{3,67},{67,3},{4,68},{68... | collective-permute-start | bytes 2515976 | tf_op jit(solution)/shard_map/ppermute | solution.py:33
  708.5 640.0 %all-reduce.9.cloned.1.call-start = ((), (), s32[]{:S(2)}) async-start(), calls=%async_computation.4 | async-start | bytes 5521408 | tf_op jit(solution)/shard_map/psum | solution.py:274
  (36 other events, 405.4 us)
Sparse Core Ops, SparseCore 0:
  708.6 555.5 all-reduce.6
  1266.8 81.7 all-reduce.8
